TPU v7x, 32 devices: a whole 2x2x4 slice. The times are simulated.
32 devices in a mesh: mp: 4 (over x, core), seq: 8 (over z, y).
Axes of the slice: x: 2, y: 2, z: 4, core: 2. Of those that a mesh axis runs over, the one named last changes fastest.
Arguments:
- hidden_in: bfloat16 [2048, 5376], P('seq', 'mp'), may hold values from -28 to 28
- gain_in: float32 [5376], replicated, may hold values from 0.3 to 3
- w_query: bfloat16 [5376, 4096], P('seq', 'mp'), may hold values from -0.078125 to 0.078125
- key_weight: bfloat16 [5376, 2048], P('seq', 'mp'), may hold values from -0.078125 to 0.078125
- value_weight: bfloat16 [5376, 2048], P('seq', 'mp'), may hold values from -0.078125 to 0.078125
- gain_query: float32 [128], replicated, may hold values from 0.3 to 3
- gain_key: float32 [128], replicated, may hold values from 0.3 to 3
- start_pos: int32 [1], replicated, may hold values from 1024 to 4095
- cached_key_rows: bfloat16 [1024, 2048], P(None, 'mp'), may hold values from -140 to 140
- cached_value_rows: bfloat16 [1024, 2048], P(None, 'mp'), may hold values from -5 to 5
- w_out: bfloat16 [4096, 5376], P('seq', 'mp'), may hold values from -1.5 to 1.5
- gain_post: float32 [5376], P('mp'), may hold values from 0.3 to 3
Outputs:
- hidden_out: bfloat16 [2048, 5376], P('seq', 'mp')
All inputs are finite; a program needn't handle non-finite values.
Results may differ from a plain program's by a relative error of at most 0.012.
The roundings to bfloat16 on the way count: a program that leaves them out, or rounds other values in their place, can miss the bound.
Values may be sent and summed in bfloat16 or wider, within the bound.
A program may use at most 128 MiB of HBM per device.

v0:
```python
import jax
import jax.numpy as jnp
from jax import lax
from jax.sharding import PartitionSpec as P

MODEL_WIDTH = 5376
WINDOW_LENGTH = 1024
epsilon = 1e-06
query_scale = 168.0 ** (-0.5)
rope_base = 10000.0


def shifted(x, axis, by):
    peers = lax.axis_size(axis)
    pairs = [(i, i + by) for i in range(peers) if 0 <= i + by < peers]
    return lax.ppermute(x, axis, pairs)


def norm_rows(values, gain):
    return values * lax.rsqrt(jnp.mean(values * values, axis=-1, keepdims=True) + epsilon) * gain


def rotate(tensor, positions):
    half_dim = tensor.shape[-1] // 2
    inverse_freq = rope_base ** (
        -(jnp.arange(half_dim, dtype=jnp.float32) * 2.0) / tensor.shape[-1]
    )
    angles = positions.astype(jnp.float32)[:, None, None] * inverse_freq[None, None, :]
    cosine = jnp.cos(angles)
    sine = jnp.sin(angles)
    first = tensor[..., :half_dim]
    second = tensor[..., half_dim:]
    return jnp.concatenate(
        [first * cosine - second * sine, second * cosine + first * sine], axis=-1
    )


def on_device(
    hidden_in,
    gain_in,
    w_query,
    key_weight,
    value_weight,
    gain_query,
    gain_key,
    start_pos,
    cached_key_rows,
    cached_value_rows,
    w_out,
    gain_post,
):
    n_rows = hidden_in.shape[0]
    head_dim = gain_query.shape[0]
    kv_cols = key_weight.shape[1]
    kv_heads = kv_cols // head_dim
    q_heads = w_query.shape[1] // head_dim
    query_group_count = q_heads // kv_heads
    full_rows = lax.all_gather(hidden_in, "mp", axis=1, tiled=True)
    normed_hidden = norm_rows(full_rows.astype(jnp.float32), gain_in).astype(jnp.bfloat16)

    def add_rows(block_rows):
        return jnp.dot(normed_hidden, block_rows, preferred_element_type=jnp.float32)

    keys_raw = add_rows(lax.all_gather(key_weight, "seq", axis=0, tiled=True))
    values_raw = add_rows(lax.all_gather(value_weight, "seq", axis=0, tiled=True))
    query_matrix = add_rows(lax.all_gather(w_query, "seq", axis=0, tiled=True))
    seq_index = lax.axis_index("seq")
    positions = start_pos[0] + seq_index * n_rows + jnp.arange(n_rows, dtype=jnp.int32)
    query_matrix = (
        rotate(norm_rows(query_matrix.reshape(n_rows, q_heads, head_dim), gain_query), positions)
        * query_scale
    ).astype(jnp.bfloat16)
    fresh_key = rotate(
        norm_rows(keys_raw.reshape(n_rows, kv_heads, head_dim), gain_key), positions
    ).astype(jnp.bfloat16)
    fresh = jnp.stack([fresh_key.reshape(n_rows, kv_cols), values_raw.astype(jnp.bfloat16)])
    reach_shards = (WINDOW_LENGTH + n_rows - 1) // n_rows
    reach_rows = reach_shards * n_rows
    pieces = []
    moving = fresh
    for hop_index in range(reach_shards):
        moving = shifted(moving, "seq", 1)
        pieces.insert(0, moving)
    prior = jnp.concatenate(pieces, axis=1)
    front_pad = reach_rows - WINDOW_LENGTH
    cached = jnp.stack([cached_key_rows, cached_value_rows])
    padded = jnp.concatenate(
        [
            jnp.zeros((2, front_pad, kv_cols), cached.dtype),
            cached,
            jnp.zeros((2, reach_rows, kv_cols), cached.dtype),
        ],
        axis=1,
    )
    cache_start = jnp.minimum(seq_index * n_rows, front_pad + WINDOW_LENGTH)
    from_cache = lax.dynamic_slice_in_dim(padded, cache_start, reach_rows, 1)
    prior_rows = jnp.arange(reach_rows, dtype=jnp.int32)
    use_cache = prior_rows < reach_rows - seq_index * n_rows
    prior = jnp.where(use_cache[None, :, None], from_cache, prior)
    window_kv = jnp.concatenate([prior, fresh], axis=1)
    span_rows = reach_rows + n_rows
    key_heads = window_kv[0].reshape(span_rows, kv_heads, head_dim)
    value_heads = window_kv[1].reshape(span_rows, kv_heads, head_dim)
    query_heads = query_matrix.reshape(n_rows, kv_heads, query_group_count, head_dim)
    scores = jnp.einsum(
        "tkgd,skd->kgts", query_heads, key_heads, preferred_element_type=jnp.float32
    )
    query_index = jnp.arange(n_rows, dtype=jnp.int32)[:, None]
    key_index = jnp.arange(span_rows, dtype=jnp.int32)[None, :]
    visible = (key_index > query_index + reach_rows - WINDOW_LENGTH) & (
        key_index <= query_index + reach_rows
    )
    scores = jnp.where(visible, scores, -jnp.inf)
    row_max = jnp.max(scores, axis=-1, keepdims=True)
    probs = jnp.exp(scores - row_max)
    totals = jnp.sum(probs, axis=-1)
    probs_b = probs.astype(jnp.bfloat16)
    summed = jnp.einsum("kgts,skd->tkgd", probs_b, value_heads, preferred_element_type=jnp.float32)
    summed = summed / jnp.transpose(totals, (2, 0, 1))[..., None]
    attn = summed.reshape(n_rows, q_heads * head_dim).astype(jnp.bfloat16)
    all_heads = lax.all_gather(attn, "mp", axis=1, tiled=True)
    projected = jnp.dot(
        all_heads,
        lax.all_gather(w_out, "seq", axis=0, tiled=True),
        preferred_element_type=jnp.float32,
    )
    squares = lax.psum(jnp.sum(projected * projected, axis=-1), "mp")
    scaling = lax.rsqrt(squares / MODEL_WIDTH + epsilon)
    return (hidden_in.astype(jnp.float32) + projected * scaling[:, None] * gain_post).astype(
        jnp.bfloat16
    )


def solution(mesh):
    in_specs = (
        P("seq", "mp"),
        P(),
        P("seq", "mp"),
        P("seq", "mp"),
        P("seq", "mp"),
        P(),
        P(),
        P(),
        P(None, "mp"),
        P(None, "mp"),
        P("seq", "mp"),
        P("mp"),
    )
    out_specs = P("seq", "mp")
    return jax.shard_map(
        on_device, mesh=mesh, in_specs=in_specs, out_specs=out_specs, check_vma=False
    )
```

profile of v0, /device:TPU:0, one launch (start us, length us, event | category | flops | bytes accessed | tf_op | source)
XLA Modules:
  0.0 618.6 jit_solution(16389566803389255011)
XLA Ops:
  6.5 0.7 all-gather.7.cloned.1.call-update
  7.3 0.7 all-gather.9.cloned.1.call-update
  11.2 26.8 %all-gather.7.cloned.1.call-done = bf16[256,5376]{0,1:T(8,128)(2,1)} async-done(((bf16[256,1344]{0,1:T(8,128)(2,1)}), bf16[256,5376]{0,1:T(8,128)(2,1)}) %all-gather.7.cloned.1.call-update) | async-done | bytes 2752528 | tf_op jit(solution)/shard_map/all_gather | solution.py:58
  37.9 2.5 fusion.3
  40.5 89.1 %all-gather.9.cloned.1.call-done = bf16[5376,512]{1,0:T(8,128)(2,1)} async-done(((bf16[672,512]{1,0:T(8,128)(2,1)}), bf16[5376,512]{1,0:T(8,128)(2,1)}) %all-gather.9.cloned.1.call-update) | async-done | bytes 5505040 | tf_op jit(solution)/shard_map/all_gather | solution.py:64
  129.6 7.3 %fusion.32 = f32[256,512]{1,0:T(8,128)} fusion(bf16[5376,512]{1,0:T(8,128)(2,1)} %all-gather.9.cloned.1.call-done, bf16[256,5376]{0,1:T(8,128)(2,1)} %all-gather.7.cloned.1.call-done, f32[5376]{0:T(1024)S(1)} %copy-done.12, f32[256]{0:T(256)S(1)} %add_rsqrt_fusion.3), kind=kOutput, calls=%fused_computation.60 | convolution fusion | flops 1414791168 | bytes 8804352 | tf_op jit(solution)/shard_map/dot_general | solution.py:62
  137.0 1.4 reshape.136
  140.1 79.4 %all-gather.11.cloned.1.call-done = bf16[5376,512]{1,0:T(8,128)(2,1)} async-done(((bf16[672,512]{1,0:T(8,128)(2,1)}), bf16[5376,512]{1,0:T(8,128)(2,1)}) %all-gather.11.cloned.1.call-update) | async-done | bytes 5505040 | tf_op jit(solution)/shard_map/all_gather | solution.py:65
  219.5 5.7 fusion.21
  225.2 0.7 copy-done.7
  226.0 2.6 collective-permute-start
  228.6 21.6 %collective-permute-done = bf16[2,256,512]{2,1,0:T(8,128)(2,1)S(1)} collective-permute-done((bf16[2,256,512]{2,1,0:T(8,128)(2,1)S(1)}, bf16[2,256,512]{2,1,0:T(8,128)(2,1)S(1)}, u32[]{:S(2)}, u32[]{:S(2)}) %collective-permute-start) | collective-permute-done | bytes 524320 | tf_op jit(solution)/shard_map/ppermute | solution.py:16
  250.2 4.4 collective-permute-start.1
  254.6 10.3 %collective-permute-done.1 = bf16[2,256,512]{2,1,0:T(8,128)(2,1)S(1)} collective-permute-done((bf16[2,256,512]{2,1,0:T(8,128)(2,1)S(1)}, bf16[2,256,512]{2,1,0:T(8,128)(2,1)S(1)}, u32[]{:S(2)}, u32[]{:S(2)}) %collective-permute-start.1) | collective-permute-done | bytes 524320 | tf_op jit(solution)/shard_map/ppermute | solution.py:16
  264.9 14.7 %collective-permute-start.2 = (bf16[2,256,512]{2,1,0:T(8,128)(2,1)S(1)}, bf16[2,256,512]{2,1,0:T(8,128)(2,1)S(1)}, u32[]{:S(2)}, u32[]{:S(2)}) collective-permute-start(bf16[2,256,512]{2,1,0:T(8,128)(2,1)S(1)} %collective-permute-done.1), channel_id=1, source_target_pairs={{0,1},{1,2},{2,3},{3,4},{4,5},{5,6},{6,7},{8,9},{9,10},{10,11},{11... | collective-permute-start | bytes 1572872 | tf_op jit(solution)/shard_map/ppermute | solution.py:16
  279.7 6.6 %collective-permute-done.2 = bf16[2,256,512]{2,1,0:T(8,128)(2,1)S(1)} collective-permute-done((bf16[2,256,512]{2,1,0:T(8,128)(2,1)S(1)}, bf16[2,256,512]{2,1,0:T(8,128)(2,1)S(1)}, u32[]{:S(2)}, u32[]{:S(2)}) %collective-permute-start.2) | collective-permute-done | bytes 524320 | tf_op jit(solution)/shard_map/ppermute | solution.py:16
  286.3 20.5 %collective-permute-start.3 = (bf16[2,256,512]{2,1,0:T(8,128)(2,1)S(1)}, bf16[2,256,512]{2,1,0:T(8,128)(2,1)S(1)}, u32[]{:S(2)}, u32[]{:S(2)}) collective-permute-start(bf16[2,256,512]{2,1,0:T(8,128)(2,1)S(1)} %collective-permute-done.2), channel_id=1, source_target_pairs={{0,1},{1,2},{2,3},{3,4},{4,5},{5,6},{6,7},{8,9},{9,10},{10,11},{11... | collective-permute-start | bytes 1572872 | tf_op jit(solution)/shard_map/ppermute | solution.py:16
  307.1 7.0 %collective-permute-done.3 = bf16[2,256,512]{2,1,0:T(8,128)(2,1)S(1)} collective-permute-done((bf16[2,256,512]{2,1,0:T(8,128)(2,1)S(1)}, bf16[2,256,512]{2,1,0:T(8,128)(2,1)S(1)}, u32[]{:S(2)}, u32[]{:S(2)}) %collective-permute-start.3) | collective-permute-done | bytes 524320 | tf_op jit(solution)/shard_map/ppermute | solution.py:16
  314.1 5.9 fusion.14
  320.2 1.3 fusion.34
  321.5 2.7 reshape_squeeze.7
  324.2 1.5 copy.37
  325.6 85.2 %all-gather.13.cloned.1.call-done = bf16[5376,1024]{1,0:T(8,128)(2,1)} async-done(((bf16[672,1024]{1,0:T(8,128)(2,1)}), bf16[5376,1024]{1,0:T(8,128)(2,1)}) %all-gather.13.cloned.1.call-update) | async-done | bytes 11010064 | tf_op jit(solution)/shard_map/all_gather | solution.py:66
  410.9 8.1 %convolution_bitcast_fusion = f32[32,8,8,128]{3,1,2,0:T(8,128)S(1)} fusion(bf16[5376,1024]{1,0:T(8,128)(2,1)} %all-gather.13.cloned.1.call-done, bf16[256,5376]{0,1:T(8,128)(2,1)} %all-gather.7.cloned.1.call-done, f32[5376]{0:T(1024)S(1)} %copy-done.13, f32[256]{0:T(256)S(1)} %add_rsqrt_fusion.3), kind=kOutput, calls=%fused_computation.27 | convolution fusion | flops 2824077312 | bytes 14833664 | tf_op jit(solution)/shard_map/dot_general | solution.py:62
  421.1 1.7 fusion
  422.9 1.8 fusion.1
  424.7 3.3 divide_convert_fusion
  428.0 147.9 %all-gather.17.cloned.1.call-done = bf16[4096,1344]{0,1:T(8,128)(2,1)} async-done(((bf16[512,1344]{0,1:T(8,128)(2,1)}), bf16[4096,1344]{0,1:T(8,128)(2,1)}) %all-gather.17.cloned.1.call-update) | async-done | bytes 11010064 | tf_op jit(solution)/shard_map/all_gather | solution.py:124
  575.9 22.2 %all-gather.15.cloned.1.call-done = bf16[256,4096]{0,1:T(8,128)(2,1)} async-done(((bf16[256,1024]{0,1:T(8,128)(2,1)}), bf16[256,4096]{0,1:T(8,128)(2,1)}) %all-gather.15.cloned.1.call-update) | async-done | bytes 2097168 | tf_op jit(solution)/shard_map/all_gather | solution.py:121
  598.1 6.4 %multiply_reduce_fusion = (f32[256]{0:T(256)S(1)}, f32[256,1344]{0,1:T(8,128)S(1)}) fusion(bf16[4096,1344]{0,1:T(8,128)(2,1)} %all-gather.17.cloned.1.call-done, bf16[256,4096]{0,1:T(8,128)(2,1)} %all-gather.15.cloned.1.call-done), kind=kOutput, calls=%fused_computation.25 | convolution fusion | flops 2819260160 | bytes 14484480 | tf_op jit(solution)/shard_map/dot_general | solution.py:122
  604.6 5.9 psum.7
  610.5 1.2 add_convert_fusion
  (62 shorter events, 6.8 us)
Async XLA Ops:
  6.5 123.1 %copy-start.12 = (f32[5376]{0:T(1024)S(1)}, f32[5376]{0:T(1024)}, u32[]{:S(2)}) copy-start(f32[5376]{0:T(1024)} %param.13) | copy-start | bytes 64516
  6.5 31.4 %all-gather.7.cloned.1.call-start = ((), (), s32[]{:S(2)}) async-start(), calls=%async_computation | async-start | bytes 3440640 | tf_op jit(solution)/shard_map/all_gather | solution.py:58
  7.3 122.4 %all-gather.9.cloned.1.call-start = ((), (), s32[]{:S(2)}) async-start(), calls=%async_computation.1 | async-start | bytes 6193152 | tf_op jit(solution)/shard_map/all_gather | solution.py:64
  8.0 211.5 %all-gather.11.cloned.1.call-start = ((), (), s32[]{:S(2)}) async-start(), calls=%async_computation.2 | async-start | bytes 6193152 | tf_op jit(solution)/shard_map/all_gather | solution.py:65
  8.7 402.1 %all-gather.13.cloned.1.call-start = ((), (), s32[]{:S(2)}) async-start(), calls=%async_computation.3 | async-start | bytes 12386304 | tf_op jit(solution)/shard_map/all_gather | solution.py:66
  9.3 566.6 %all-gather.17.cloned.1.call-start = ((), (), s32[]{:S(2)}) async-start(), calls=%async_computation.5 | async-start | bytes 12386304 | tf_op jit(solution)/shard_map/all_gather | solution.py:124
  9.9 588.2 %all-gather.15.cloned.1.call-start = ((), (), s32[]{:S(2)}) async-start(), calls=%async_computation.4 | async-start | bytes 2621440 | tf_op jit(solution)/shard_map/all_gather | solution.py:121
  11.2 127.9 %copy-start.3 = (f32[256,64]{1,0:T(8,128)}, f32[256,64]{1,0:T(8,128)S(1)}, u32[]{:S(2)}) copy-start(f32[256,64]{1,0:T(8,128)S(1)} %get-tuple-element.11) | copy-start | bytes 196612
  11.2 127.9 %copy-start.5 = (f32[256,64]{1,0:T(8,128)}, f32[256,64]{1,0:T(8,128)S(1)}, u32[]{:S(2)}) copy-start(f32[256,64]{1,0:T(8,128)S(1)} %get-tuple-element.12) | copy-start | bytes 196612
  40.5 98.3 %copy-start.10 = (f32[128]{0:T(128)S(1)}, f32[128]{0:T(128)}, u32[]{:S(2)}) copy-start(f32[128]{0:T(128)} %param.18) | copy-start | bytes 1540
  137.0 82.6 %copy-start = (bf16[256,5376]{0,1:T(8,128)(2,1)S(1)}, bf16[256,5376]{0,1:T(8,128)(2,1)}, u32[]{:S(2)}) copy-start(bf16[256,5376]{0,1:T(8,128)(2,1)} %all-gather.7.cloned.1.call-done) | copy-start | bytes 8257540
  225.2 0.7 copy-start.7
  226.0 94.1 %copy-start.8 = (bf16[1,256,512]{2,1,0:T(8,128)(2,1)S(1)}, bf16[1,256,512]{2,1,0:T(8,128)(2,1)}, u32[]{:S(2)}) copy-start(bf16[1,256,512]{2,1,0:T(8,128)(2,1)} %copy-done.7) | copy-start | bytes 786436
  226.0 24.2 %collective-permute-start = (bf16[2,256,512]{2,1,0:T(8,128)(2,1)S(1)}, bf16[2,256,512]{2,1,0:T(8,128)(2,1)S(1)}, u32[]{:S(2)}, u32[]{:S(2)}) collective-permute-start(bf16[2,256,512]{2,1,0:T(8,128)(2,1)S(1)} %pad_maximum_fusion), channel_id=1, source_target_pairs={{0,1},{1,2},{2,3},{3,4},{4,5},{5,6},{6,7},{8,9},{9,10},{10,11},{11... | collective-permute-start | bytes 1572872 | tf_op jit(solution)/shard_map/ppermute | solution.py:16
  250.2 14.7 %collective-permute-start.1 = (bf16[2,256,512]{2,1,0:T(8,128)(2,1)S(1)}, bf16[2,256,512]{2,1,0:T(8,128)(2,1)S(1)}, u32[]{:S(2)}, u32[]{:S(2)}) collective-permute-start(bf16[2,256,512]{2,1,0:T(8,128)(2,1)S(1)} %collective-permute-done), channel_id=1, source_target_pairs={{0,1},{1,2},{2,3},{3,4},{4,5},{5,6},{6,7},{8,9},{9,10},{10,11},{11... | collective-permute-start | bytes 1572872 | tf_op jit(solution)/shard_map/ppermute | solution.py:16
  264.9 21.4 %collective-permute-start.2 = (bf16[2,256,512]{2,1,0:T(8,128)(2,1)S(1)}, bf16[2,256,512]{2,1,0:T(8,128)(2,1)S(1)}, u32[]{:S(2)}, u32[]{:S(2)}) collective-permute-start(bf16[2,256,512]{2,1,0:T(8,128)(2,1)S(1)} %collective-permute-done.1), channel_id=1, source_target_pairs={{0,1},{1,2},{2,3},{3,4},{4,5},{5,6},{6,7},{8,9},{9,10},{10,11},{11... | collective-permute-start | bytes 1572872 | tf_op jit(solution)/shard_map/ppermute | solution.py:16
  286.3 27.8 %collective-permute-start.3 = (bf16[2,256,512]{2,1,0:T(8,128)(2,1)S(1)}, bf16[2,256,512]{2,1,0:T(8,128)(2,1)S(1)}, u32[]{:S(2)}, u32[]{:S(2)}) collective-permute-start(bf16[2,256,512]{2,1,0:T(8,128)(2,1)S(1)} %collective-permute-done.2), channel_id=1, source_target_pairs={{0,1},{1,2},{2,3},{3,4},{4,5},{5,6},{6,7},{8,9},{9,10},{10,11},{11... | collective-permute-start | bytes 1572872 | tf_op jit(solution)/shard_map/ppermute | solution.py:16
  320.2 90.7 %copy-start.13 = (f32[5376]{0:T(1024)S(1)}, f32[5376]{0:T(1024)}, u32[]{:S(2)}) copy-start(f32[5376]{0:T(1024)} %param.13) | copy-start | bytes 64516
  325.6 94.1 %copy-start.11 = (f32[128]{0:T(128)S(1)}, f32[128]{0:T(128)}, u32[]{:S(2)}) copy-start(f32[128]{0:T(128)} %param.17) | copy-start | bytes 1540
  418.9 1.1 copy-start.4
  419.0 1.1 copy-start.6
  422.9 1.8 copy-start.2
  428.0 182.5 %copy-start.1 = (bf16[256,1344]{0,1:T(8,128)(2,1)S(1)}, bf16[256,1344]{0,1:T(8,128)(2,1)}, u32[]{:S(2)}) copy-start(bf16[256,1344]{0,1:T(8,128)(2,1)} %param.12) | copy-start | bytes 2064388
  428.0 182.5 %copy-start.9 = (f32[1344]{0:T(1024)S(1)}, f32[1344]{0:T(1024)}, u32[]{:S(2)}) copy-start(f32[1344]{0:T(1024)} %param.23) | copy-start | bytes 16132
Sparse Core Ops, SparseCore 0:
  8.9 28.9 all-gather.6
  40.1 89.4 all-gather.8
  131.8 87.6 all-gather.10
  221.5 189.2 all-gather.12
  412.7 163.1 all-gather.16
  577.3 20.7 all-gather.14
where the time goes:
time: 619 us
  waiting for transfers between devices  499 us (81%)
  starting transfers between devices  42.4 us (7%)
  matrix products  32.6 us (5%)
  other arithmetic  15.4 us (2%)
  between operations  14.5 us (2%)
  local copies, waits for them, and re-layouts  8.49 us (1%)
    all_gather x1, waiting for transfers between devices, on_device(): lax.all_gather(w_out, 'seq', axis=0, tiled=True)  148 us
    all_gather x1, waiting for transfers between devices, on_device(): keys_raw = add_rows(lax.all_gather(key_weight, 'seq', axis=0, tiled=True))  89.1 us
    all_gather x1, waiting for transfers between devices, on_device(): query_matrix = add_rows(lax.all_gather(w_query, 'seq', axis=0, tiled=True))  85.2 us
    all_gather x1, waiting for transfers between devices, on_device(): lax.all_gather(value_weight, 'seq', axis=0, tiled=True)  79.4 us
    ppermute x4, waiting for transfers between devices, shifted(): return lax.ppermute(x, axis, pairs)  45.6 us
    ppermute x4, starting transfers between devices, shifted(): return lax.ppermute(x, axis, pairs)  42.2 us
    all_gather x1, waiting for transfers between devices, on_device(): full_rows = lax.all_gather(hidden_in, 'mp', axis=1, tiled=True)  26.8 us
    all_gather x1, waiting for transfers between devices, on_device(): all_heads = lax.all_gather(attn, 'mp', axis=1, tiled=True)  22.2 us
  transfers between devices with their start and end apart: 10, of which 10 were waited for; matrix products, arithmetic and copies ran while one was open for 8% of the time, Pallas kernels for 0%

commit v1 on v0

--- a/solution.py
+++ b/solution.py
@@ -55,7 +55,19 @@
     kv_heads = kv_cols // head_dim
     q_heads = w_query.shape[1] // head_dim
     query_group_count = q_heads // kv_heads
-    full_rows = lax.all_gather(hidden_in, "mp", axis=1, tiled=True)
+    n_parts = lax.axis_size("mp")
+    z = sorted(((w, (w + 1) % n_parts) for w in range(n_parts)))
+    r1 = hidden_in
+    cards = [r1]
+    idx = 1
+    while idx < n_parts:
+        r1 = lax.ppermute(r1, "mp", z)
+        cards.insert(0, r1)
+        idx = idx + 1
+    out_arr = jnp.concatenate(cards, axis=1)
+    upper = lax.axis_index("mp")
+    lower = upper + 1
+    full_rows = jnp.roll(out_arr, lower * hidden_in.shape[1], axis=1)
     normed_hidden = norm_rows(full_rows.astype(jnp.float32), gain_in).astype(jnp.bfloat16)
 
     def add_rows(block_rows):

time: 619 us -> 591 us (0.955)
  waiting for transfers between devices: 499 us -> 466 us
    all_gather x1, waiting for transfers between devices: 89.1 us -> 56.5 us  [on_device(): keys_raw = add_rows(lax.all_gather(key_weight, 'seq', axis=0, tiled=True))]
    ppermute x0 -> x3, waiting for transfers between devices: none -> 30.2 us  [on_device(): r1 = lax.ppermute(r1, 'mp', z)]
    all_gather x1 -> x0, waiting for transfers between devices: 26.8 us -> none  [on_device(): full_rows = lax.all_gather(hidden_in, 'mp', axis=1, tiled=True)]
  transfers between devices with their start and end apart: 10 -> 12, of which waited for: 10 -> 12; matrix products, arithmetic and copies ran while one was open for 8% -> 9% of each run, Pallas kernels for 0% -> 0%
where the time goes in v1:
time: 591 us
  waiting for transfers between devices  466 us (79%)
  starting transfers between devices  44.1 us (7%)
  matrix products  32.7 us (6%)
  other arithmetic  15.7 us (3%)
  between operations  14.1 us (2%)
  local copies, waits for them, and re-layouts  12.4 us (2%)
    all_gather x1, waiting for transfers between devices, on_device(): lax.all_gather(w_out, 'seq', axis=0, tiled=True)  142 us
    all_gather x1, waiting for transfers between devices, on_device(): query_matrix = add_rows(lax.all_gather(w_query, 'seq', axis=0, tiled=True))  84.6 us
    all_gather x1, waiting for transfers between devices, on_device(): lax.all_gather(value_weight, 'seq', axis=0, tiled=True)  81.4 us
    all_gather x1, waiting for transfers between devices, on_device(): keys_raw = add_rows(lax.all_gather(key_weight, 'seq', axis=0, tiled=True))  56.5 us
    ppermute x4, waiting for transfers between devices, shifted(): return lax.ppermute(x, axis, pairs)  45.8 us
    ppermute x4, starting transfers between devices, shifted(): return lax.ppermute(x, axis, pairs)  43.4 us
    ppermute x3, waiting for transfers between devices, on_device(): r1 = lax.ppermute(r1, 'mp', z)  30.2 us
    all_gather x1, waiting for transfers between devices, on_device(): all_heads = lax.all_gather(attn, 'mp', axis=1, tiled=True)  22.2 us
  transfers between devices with their start and end apart: 12, of which 12 were waited for; matrix products, arithmetic and copies ran while one was open for 9% of the time, Pallas kernels for 0%

profile of v1, /device:TPU:0, one launch (start us, length us, event | category | flops | bytes accessed | tf_op | source)
XLA Modules:
  0.0 590.6 jit_solution(4013019380662077168)
XLA Ops:
  9.9 10.8 %collective-permute-done = bf16[256,1344]{0,1:T(8,128)(2,1)S(1)} collective-permute-done((bf16[256,1344]{0,1:T(8,128)(2,1)}, bf16[256,1344]{0,1:T(8,128)(2,1)S(1)}, u32[]{:S(2)}, u32[]{:S(2)}) %collective-permute-start) | collective-permute-done | bytes 688160 | tf_op jit(solution)/shard_map/ppermute | solution.py:64
  20.7 10.3 %collective-permute-done.1 = bf16[256,1344]{0,1:T(8,128)(2,1)S(1)} collective-permute-done((bf16[256,1344]{0,1:T(8,128)(2,1)S(1)}, bf16[256,1344]{0,1:T(8,128)(2,1)S(1)}, u32[]{:S(2)}, u32[]{:S(2)}) %collective-permute-start.1) | collective-permute-done | bytes 688160 | tf_op jit(solution)/shard_map/ppermute | solution.py:64
  32.2 9.1 %collective-permute-done.2 = bf16[256,1344]{0,1:T(8,128)(2,1)S(1)} collective-permute-done((bf16[256,1344]{0,1:T(8,128)(2,1)S(1)}, bf16[256,1344]{0,1:T(8,128)(2,1)S(1)}, u32[]{:S(2)}, u32[]{:S(2)}) %collective-permute-start.2) | collective-permute-done | bytes 688160 | tf_op jit(solution)/shard_map/ppermute | solution.py:64
  41.8 2.4 copy-done.1
  45.2 56.5 %all-gather.6.cloned.1.call-done = bf16[5376,512]{1,0:T(8,128)(2,1)} async-done(((bf16[672,512]{1,0:T(8,128)(2,1)}), bf16[5376,512]{1,0:T(8,128)(2,1)}) %all-gather.6.cloned.1.call-update) | async-done | bytes 5505040 | tf_op jit(solution)/shard_map/all_gather | solution.py:76
  101.7 6.5 %fusion.32 = f32[256,512]{1,0:T(8,128)S(1)} fusion(bf16[5376,512]{1,0:T(8,128)(2,1)} %all-gather.6.cloned.1.call-done, f32[5376]{0:T(1024)S(1)} %copy-done.8, f32[256]{0:T(256)S(1)} %add_rsqrt_fusion.3, bf16[256,10752]{0,1:T(8,128)(2,1)} %copy-done.1, s32[]{:T(128)S(6)} %select_n.26), kind=kOutput, calls=%fused_computation.68 | convolution fusion | flops 1414791168 | bytes 8804356 | tf_op jit(solution)/shard_map/dot_general | solution.py:74
  110.2 81.4 %all-gather.8.cloned.1.call-done = bf16[5376,512]{1,0:T(8,128)(2,1)} async-done(((bf16[672,512]{1,0:T(8,128)(2,1)}), bf16[5376,512]{1,0:T(8,128)(2,1)}) %all-gather.8.cloned.1.call-update) | async-done | bytes 5505040 | tf_op jit(solution)/shard_map/all_gather | solution.py:77
  191.6 6.5 %fusion.21 = bf16[1,256,512]{2,1,0:T(8,128)(2,1)S(1)} fusion(bf16[5376,512]{1,0:T(8,128)(2,1)} %all-gather.8.cloned.1.call-done, f32[5376]{0:T(1024)S(1)} %copy-done.8, f32[256]{0:T(256)S(1)} %add_rsqrt_fusion.3, bf16[256,10752]{0,1:T(8,128)(2,1)} %copy-done.1, s32[]{:T(128)S(6)} %select_n.26), kind=kOutput, calls=%fused_computation.32 | convolution fusion | flops 1414922240 | bytes 8542212 | tf_op jit(solution)/shard_map/dot_general | solution.py:74
  198.2 2.5 collective-permute-start.3
  200.7 21.6 %collective-permute-done.3 = bf16[2,256,512]{2,1,0:T(8,128)(2,1)S(1)} collective-permute-done((bf16[2,256,512]{2,1,0:T(8,128)(2,1)S(1)}, bf16[2,256,512]{2,1,0:T(8,128)(2,1)S(1)}, u32[]{:S(2)}, u32[]{:S(2)}) %collective-permute-start.3) | collective-permute-done | bytes 524320 | tf_op jit(solution)/shard_map/ppermute | solution.py:16
  222.3 5.2 collective-permute-start.4
  227.5 9.6 %collective-permute-done.4 = bf16[2,256,512]{2,1,0:T(8,128)(2,1)} collective-permute-done((bf16[2,256,512]{2,1,0:T(8,128)(2,1)S(1)}, bf16[2,256,512]{2,1,0:T(8,128)(2,1)}, u32[]{:S(2)}, u32[]{:S(2)}) %collective-permute-start.4) | collective-permute-done | bytes 524320 | tf_op jit(solution)/shard_map/ppermute | solution.py:16
  237.1 15.3 %collective-permute-start.5 = (bf16[2,256,512]{2,1,0:T(8,128)(2,1)}, bf16[2,256,512]{2,1,0:T(8,128)(2,1)}, u32[]{:S(2)}, u32[]{:S(2)}) collective-permute-start(bf16[2,256,512]{2,1,0:T(8,128)(2,1)} %collective-permute-done.4), channel_id=1, source_target_pairs={{0,1},{1,2},{2,3},{3,4},{4,5},{5,6},{6,7},{8,9},{9,10},{10,11},{11... | collective-permute-start | bytes 1572872 | tf_op jit(solution)/shard_map/ppermute | solution.py:16
  252.3 6.2 %collective-permute-done.5 = bf16[2,256,512]{2,1,0:T(8,128)(2,1)} collective-permute-done((bf16[2,256,512]{2,1,0:T(8,128)(2,1)}, bf16[2,256,512]{2,1,0:T(8,128)(2,1)}, u32[]{:S(2)}, u32[]{:S(2)}) %collective-permute-start.5) | collective-permute-done | bytes 524320 | tf_op jit(solution)/shard_map/ppermute | solution.py:16
  258.5 20.5 %collective-permute-start.6 = (bf16[2,256,512]{2,1,0:T(8,128)(2,1)}, bf16[2,256,512]{2,1,0:T(8,128)(2,1)S(1)}, u32[]{:S(2)}, u32[]{:S(2)}) collective-permute-start(bf16[2,256,512]{2,1,0:T(8,128)(2,1)} %collective-permute-done.5), channel_id=1, source_target_pairs={{0,1},{1,2},{2,3},{3,4},{4,5},{5,6},{6,7},{8,9},{9,10},{10,11},{11... | collective-permute-start | bytes 1572872 | tf_op jit(solution)/shard_map/ppermute | solution.py:16
  279.3 8.5 %collective-permute-done.6 = bf16[2,256,512]{2,1,0:T(8,128)(2,1)S(1)} collective-permute-done((bf16[2,256,512]{2,1,0:T(8,128)(2,1)}, bf16[2,256,512]{2,1,0:T(8,128)(2,1)S(1)}, u32[]{:S(2)}, u32[]{:S(2)}) %collective-permute-start.6) | collective-permute-done | bytes 524320 | tf_op jit(solution)/shard_map/ppermute | solution.py:16
  287.7 5.5 fusion.14
  293.4 1.8 fusion.34
  295.2 2.7 reshape_squeeze.7
  297.9 2.4 copy.37
  300.3 84.6 %all-gather.10.cloned.1.call-done = bf16[5376,1024]{1,0:T(8,128)(2,1)} async-done(((bf16[672,1024]{1,0:T(8,128)(2,1)}), bf16[5376,1024]{1,0:T(8,128)(2,1)}) %all-gather.10.cloned.1.call-update) | async-done | bytes 11010064 | tf_op jit(solution)/shard_map/all_gather | solution.py:78
  384.9 8.1 %convolution_bitcast_fusion = f32[32,8,8,128]{3,1,2,0:T(8,128)S(1)} fusion(bf16[5376,1024]{1,0:T(8,128)(2,1)} %all-gather.10.cloned.1.call-done, f32[5376]{0:T(1024)S(1)} %copy-done.8, f32[256]{0:T(256)S(1)} %add_rsqrt_fusion.3, bf16[256,10752]{0,1:T(8,128)(2,1)} %copy-done.1, s32[]{:T(128)S(6)} %select_n.26), kind=kOutput, calls=%fused_computation.27 | convolution fusion | flops 2824077312 | bytes 14833668 | tf_op jit(solution)/shard_map/dot_general | solution.py:74
  396.0 1.2 multiply_multiply_fusion
  397.2 1.3 multiply_subtract_fusion
  399.0 1.7 fusion
  400.7 1.8 fusion.1
  402.5 3.3 divide_convert_fusion
  405.9 142.4 %all-gather.14.cloned.1.call-done = bf16[4096,1344]{0,1:T(8,128)(2,1)} async-done(((bf16[512,1344]{0,1:T(8,128)(2,1)}), bf16[4096,1344]{0,1:T(8,128)(2,1)}) %all-gather.14.cloned.1.call-update) | async-done | bytes 11010064 | tf_op jit(solution)/shard_map/all_gather | solution.py:136
  548.2 22.2 %all-gather.12.cloned.1.call-done = bf16[256,4096]{0,1:T(8,128)(2,1)} async-done(((bf16[256,1024]{0,1:T(8,128)(2,1)}), bf16[256,4096]{0,1:T(8,128)(2,1)}) %all-gather.12.cloned.1.call-update) | async-done | bytes 2097168 | tf_op jit(solution)/shard_map/all_gather | solution.py:133
  570.5 6.4 %multiply_reduce_fusion = (f32[256]{0:T(256)S(1)}, f32[256,1344]{0,1:T(8,128)S(1)}) fusion(bf16[4096,1344]{0,1:T(8,128)(2,1)} %all-gather.14.cloned.1.call-done, bf16[256,4096]{0,1:T(8,128)(2,1)} %all-gather.12.cloned.1.call-done), kind=kOutput, calls=%fused_computation.25 | convolution fusion | flops 2819260160 | bytes 14484480 | tf_op jit(solution)/shard_map/dot_general | solution.py:134
  576.9 5.9 psum.7
  582.8 1.2 add_convert_fusion
  (63 shorter events, 11.0 us)
Async XLA Ops:
  6.5 35.0 %copy-start = (bf16[256,1344]{0,1:T(8,128)(2,1)S(1)}, bf16[256,1344]{0,1:T(8,128)(2,1)}, u32[]{:S(2)}) copy-start(bf16[256,1344]{0,1:T(8,128)(2,1)} %param.12) | copy-start | bytes 2064388
  6.5 95.2 %all-gather.6.cloned.1.call-start = ((), (), s32[]{:S(2)}) async-start(), calls=%async_computation | async-start | bytes 6193152 | tf_op jit(solution)/shard_map/all_gather | solution.py:76
  7.3 184.3 %all-gather.8.cloned.1.call-start = ((), (), s32[]{:S(2)}) async-start(), calls=%async_computation.1 | async-start | bytes 6193152 | tf_op jit(solution)/shard_map/all_gather | solution.py:77
  8.0 376.9 %all-gather.10.cloned.1.call-start = ((), (), s32[]{:S(2)}) async-start(), calls=%async_computation.2 | async-start | bytes 12386304 | tf_op jit(solution)/shard_map/all_gather | solution.py:78
  8.7 539.5 %all-gather.14.cloned.1.call-start = ((), (), s32[]{:S(2)}) async-start(), calls=%async_computation.4 | async-start | bytes 12386304 | tf_op jit(solution)/shard_map/all_gather | solution.py:136
  9.3 561.1 %all-gather.12.cloned.1.call-start = ((), (), s32[]{:S(2)}) async-start(), calls=%async_computation.3 | async-start | bytes 2621440 | tf_op jit(solution)/shard_map/all_gather | solution.py:133
  9.4 11.3 %collective-permute-start = (bf16[256,1344]{0,1:T(8,128)(2,1)}, bf16[256,1344]{0,1:T(8,128)(2,1)S(1)}, u32[]{:S(2)}, u32[]{:S(2)}) collective-permute-start(bf16[256,1344]{0,1:T(8,128)(2,1)} %param.12), channel_id=1, source_target_pairs={{0,8},{8,16},{16,24},{24,0},{1,9},{9,17},{17,25},{25,1},{2,10},{10... | collective-permute-start | bytes 2064392 | tf_op jit(solution)/shard_map/ppermute | solution.py:64
  20.6 10.4 %collective-permute-start.1 = (bf16[256,1344]{0,1:T(8,128)(2,1)S(1)}, bf16[256,1344]{0,1:T(8,128)(2,1)S(1)}, u32[]{:S(2)}, u32[]{:S(2)}) collective-permute-start(bf16[256,1344]{0,1:T(8,128)(2,1)S(1)} %collective-permute-done), channel_id=1, source_target_pairs={{0,8},{8,16},{16,24},{24,0},{1,9},{9,17},{17,25},{25,1},{2,10},{10... | collective-permute-start | bytes 2064392 | tf_op jit(solution)/shard_map/ppermute | solution.py:64
  31.0 10.4 %collective-permute-start.2 = (bf16[256,1344]{0,1:T(8,128)(2,1)S(1)}, bf16[256,1344]{0,1:T(8,128)(2,1)S(1)}, u32[]{:S(2)}, u32[]{:S(2)}) collective-permute-start(bf16[256,1344]{0,1:T(8,128)(2,1)S(1)} %collective-permute-done.1), channel_id=1, source_target_pairs={{0,8},{8,16},{16,24},{24,0},{1,9},{9,17},{17,25},{25,1},{2,10},{10... | collective-permute-start | bytes 2064392 | tf_op jit(solution)/shard_map/ppermute | solution.py:64
  32.2 77.0 %copy-start.3 = (f32[256,64]{1,0:T(8,128)}, f32[256,64]{1,0:T(8,128)S(1)}, u32[]{:S(2)}) copy-start(f32[256,64]{1,0:T(8,128)S(1)} %get-tuple-element.12) | copy-start | bytes 196612
  41.5 60.3 %copy-start.8 = (f32[5376]{0:T(1024)S(1)}, f32[5376]{0:T(1024)}, u32[]{:S(2)}) copy-start(f32[5376]{0:T(1024)} %param.13) | copy-start | bytes 64516
  41.8 2.4 copy-start.1
  45.2 63.6 %copy-start.6 = (f32[128]{0:T(128)S(1)}, f32[128]{0:T(128)}, u32[]{:S(2)}) copy-start(f32[128]{0:T(128)} %param.18) | copy-start | bytes 1540
  110.2 177.5 %copy-start.4 = (bf16[1024,512]{1,0:T(8,128)(2,1)S(1)}, bf16[1024,512]{1,0:T(8,128)(2,1)}, u32[]{:S(2)}) copy-start(bf16[1024,512]{1,0:T(8,128)(2,1)} %param.20) | copy-start | bytes 3145732
  198.2 24.1 %collective-permute-start.3 = (bf16[2,256,512]{2,1,0:T(8,128)(2,1)S(1)}, bf16[2,256,512]{2,1,0:T(8,128)(2,1)S(1)}, u32[]{:S(2)}, u32[]{:S(2)}) collective-permute-start(bf16[2,256,512]{2,1,0:T(8,128)(2,1)S(1)} %pad_maximum_fusion), channel_id=1, source_target_pairs={{0,1},{1,2},{2,3},{3,4},{4,5},{5,6},{6,7},{8,9},{9,10},{10,11},{11... | collective-permute-start | bytes 1572872 | tf_op jit(solution)/shard_map/ppermute | solution.py:16
  222.3 14.7 %collective-permute-start.4 = (bf16[2,256,512]{2,1,0:T(8,128)(2,1)S(1)}, bf16[2,256,512]{2,1,0:T(8,128)(2,1)}, u32[]{:S(2)}, u32[]{:S(2)}) collective-permute-start(bf16[2,256,512]{2,1,0:T(8,128)(2,1)S(1)} %collective-permute-done.3), channel_id=1, source_target_pairs={{0,1},{1,2},{2,3},{3,4},{4,5},{5,6},{6,7},{8,9},{9,10},{10,11},{11... | collective-permute-start | bytes 1572872 | tf_op jit(solution)/shard_map/ppermute | solution.py:16
  237.1 21.5 %collective-permute-start.5 = (bf16[2,256,512]{2,1,0:T(8,128)(2,1)}, bf16[2,256,512]{2,1,0:T(8,128)(2,1)}, u32[]{:S(2)}, u32[]{:S(2)}) collective-permute-start(bf16[2,256,512]{2,1,0:T(8,128)(2,1)} %collective-permute-done.4), channel_id=1, source_target_pairs={{0,1},{1,2},{2,3},{3,4},{4,5},{5,6},{6,7},{8,9},{9,10},{10,11},{11... | collective-permute-start | bytes 1572872 | tf_op jit(solution)/shard_map/ppermute | solution.py:16
  258.5 29.2 %collective-permute-start.6 = (bf16[2,256,512]{2,1,0:T(8,128)(2,1)}, bf16[2,256,512]{2,1,0:T(8,128)(2,1)S(1)}, u32[]{:S(2)}, u32[]{:S(2)}) collective-permute-start(bf16[2,256,512]{2,1,0:T(8,128)(2,1)} %collective-permute-done.5), channel_id=1, source_target_pairs={{0,1},{1,2},{2,3},{3,4},{4,5},{5,6},{6,7},{8,9},{9,10},{10,11},{11... | collective-permute-start | bytes 1572872 | tf_op jit(solution)/shard_map/ppermute | solution.py:16
  300.3 95.7 %copy-start.7 = (f32[128]{0:T(128)S(1)}, f32[128]{0:T(128)}, u32[]{:S(2)}) copy-start(f32[128]{0:T(128)} %param.17) | copy-start | bytes 1540
  400.7 1.8 copy-start.2
  405.9 177.0 %copy-start.5 = (f32[1344]{0:T(1024)S(1)}, f32[1344]{0:T(1024)}, u32[]{:S(2)}) copy-start(f32[1344]{0:T(1024)} %param.23) | copy-start | bytes 16132
Sparse Core Ops, SparseCore 0:
  9.5 92.1 all-gather.5
  103.9 87.6 all-gather.7
  193.8 191.0 all-gather.9
  386.8 161.3 all-gather.13
  549.6 20.7 all-gather.11
